TPU v7x, 256 devices: a whole 4x4x8 slice. The times are simulated.
256 devices in a mesh: sub: 32 (over x, z), col: 8 (over y, core).
Axes of the slice: x: 4, y: 4, z: 8, core: 2. Of those that a mesh axis runs over, the one named last changes fastest.
Arguments:
- trace_start: bfloat16 [32, 8, 1536, 128], P('sub', 'col'), may hold values from -6 to 6
- neumann_load: bfloat16 [32, 8, 1536, 128], P('sub', 'col'), may hold values from -6 to 6
- double_layer: bfloat16 [32, 8, 1536, 1536], P('sub', 'col'), may hold values from -0.15625 to 0.15625
- single_inverse: bfloat16 [32, 8, 1536, 1536], P('sub', 'col'), may hold values from -0.15625 to 0.15625
- interface_nodes: int32 [32, 8, 8, 128], P('sub', 'col'), may hold values from -1 to 1023, as said below
- node_mode: int32 [32, 8, 1536], P('sub', 'col'), may hold values from 0 to 63
- mode_weight: bfloat16 [32, 8, 1536], P('sub', 'col'), may hold values from 0.5 to 1.5
- coarse_inverse: bfloat16 [16384, 16384], P('sub', 'col'), may hold values from -0.005859375 to 0.005859375
Outputs:
- final_trace: bfloat16 [32, 8, 1536, 128], P('sub', 'col')
- final_residual: bfloat16 [32, 8, 1536, 128], P('sub', 'col')
Inputs may be any that keep to these rules, and one draw needn't show every extreme that they name: `interface_nodes`: entry k of block (s, d) is a boundary node of s, within nodes d * 128 to (d + 1) * 128 - 1, distinct within the block, and matches entry k of the neighbour's block for direction 7 - d; valid entries come first and the rest are -1; blocks toward outside the grid are all -1; blocks of directions 1, 3, 4, 6 have 128 / 2 to 128 valid entries, the others 1 to 16, and some block has 128.
All inputs are finite; a program needn't handle non-finite values.
Results may differ from a plain program's by a relative error of at most 0.019.
Values may be sent and summed in bfloat16 or wider, within the bound.
A program may use at most 64 MiB of HBM per device.

v0:
```python
import jax
import jax.numpy as jnp
from jax import lax
from jax.sharding import PartitionSpec as P

MODES = 64
ITERS = 3
DIRECTIONS = ((-1, -1), (-1, 0), (-1, 1), (0, -1), (0, 1), (1, -1), (1, 0), (1, 1))


def from_behind(value, axis, by):
    devices = lax.axis_size(axis)
    pairs = [(i, i + by) for i in range(devices) if 0 <= i + by < devices]
    return lax.ppermute(value, axis, pairs)


def deliver_single(outgoing):
    arrivals = []
    for toward in range(8):
        row_step, col_step = DIRECTIONS[toward]
        message = outgoing[7 - toward]
        if row_step != 0:
            message = from_behind(message, "sub", -row_step)
        if col_step != 0:
            message = from_behind(message, "col", -col_step)
        arrivals.append(message)
    return jnp.stack(arrivals)


def local(
    trace_start,
    neumann_load,
    double_layer,
    single_inverse,
    interface_nodes,
    node_mode,
    mode_weight,
    coarse_inverse,
):
    trace_now = trace_start[0, 0]
    load_block = neumann_load[0, 0].astype(jnp.float32)
    kernel = double_layer[0, 0]
    inverse = single_inverse[0, 0]
    node_count = kernel.shape[0]
    interface = interface_nodes[0, 0]
    slot_count = interface.shape[1]
    band_rows = 8 * slot_count
    local_index = interface - (jnp.arange(8, dtype=jnp.int32) * slot_count)[:, None]
    selector = (
        local_index[:, :, None] == jnp.arange(slot_count, dtype=jnp.int32)[None, None, :]
    ).astype(jnp.bfloat16)
    mode_basis = jnp.where(
        node_mode[0, 0][None, :] == jnp.arange(MODES, dtype=jnp.int32)[:, None],
        mode_weight[0, 0][None, :],
        jnp.zeros((), jnp.bfloat16),
    )
    rhs_count = trace_now.shape[1]
    residual = trace_now
    rest_zeros = jnp.zeros((node_count - band_rows, rhs_count), jnp.float32)
    for iteration in range(ITERS):
        mixed_trace = (
            0.5 * trace_now.astype(jnp.float32)
            + jnp.dot(kernel, trace_now, preferred_element_type=jnp.float32)
        ).astype(jnp.bfloat16)
        flux_now = jnp.dot(inverse, mixed_trace, preferred_element_type=jnp.float32).astype(
            jnp.bfloat16
        )
        banded = flux_now[:band_rows].reshape(8, slot_count, rhs_count)
        outgoing = jnp.einsum(
            "dpq,dqr->dpr", selector, banded, preferred_element_type=jnp.float32
        ).astype(jnp.bfloat16)
        received = deliver_single(outgoing)
        placed = jnp.einsum(
            "dpq,dpr->dqr", selector, received, preferred_element_type=jnp.float32
        ).reshape(band_rows, rhs_count)
        assembled = flux_now.astype(jnp.float32) + jnp.concatenate([placed, rest_zeros], axis=0)
        residual = (load_block - assembled).astype(jnp.bfloat16)
        residual = lax.optimization_barrier(residual)
        coarse_rhs = jnp.dot(mode_basis, residual, preferred_element_type=jnp.float32).astype(
            jnp.bfloat16
        )
        partial_value = jnp.dot(
            coarse_inverse,
            lax.all_gather(coarse_rhs, "sub", axis=0, tiled=True),
            preferred_element_type=jnp.float32,
        )
        coarse_out = lax.psum_scatter(
            partial_value.astype(jnp.bfloat16), "col", scatter_dimension=0, tiled=True
        )
        correction = lax.dot_general(
            mode_basis, coarse_out, (((0,), (0,)), ((), ())), preferred_element_type=jnp.float32
        )
        trace_now = (
            trace_now.astype(jnp.float32) + 0.25 * residual.astype(jnp.float32) + correction
        ).astype(jnp.bfloat16)
    return (trace_now[None, None], residual[None, None])


def solution(mesh):
    placed = (
        P("sub", "col", None, None),
        P("sub", "col", None, None),
        P("sub", "col", None, None),
        P("sub", "col", None, None),
        P("sub", "col", None, None),
        P("sub", "col", None),
        P("sub", "col", None),
        P("sub", "col"),
    )
    return jax.shard_map(
        local,
        mesh=mesh,
        in_specs=placed,
        out_specs=(P("sub", "col", None, None), P("sub", "col", None, None)),
        check_vma=False,
    )
```

profile of v0, /device:TPU:2, one launch (start us, length us, event | category | flops | bytes accessed | tf_op | source)
XLA Modules:
  0.0 430.3 jit_solution(12199868396667985276)
XLA Ops:
  7.2 1.3 copy.26
  8.6 7.1 %fusion.54 = bf16[1536,128]{0,1:T(8,128)(2,1)S(1)} fusion(bf16[1,1,1536,1536]{3,2,1,0:T(8,128)(2,1)} %param.11, bf16[1,1,1536,1536]{3,2,1,0:T(8,128)(2,1)} %param.10, bf16[1,1,1536,128]{3,2,1,0:T(8,128)(2,1)} %param.8, bf16[1,1,1536,128]{2,3,1,0:T(8,128)(2,1)S(1)} %copy.26), kind=kOutput, calls=%fused_computation.31 | convolution fusion | flops 1208942592 | bytes 10616832 | tf_op jit(solution)/shard_map/dot_general | solution.py:65
  16.3 3.8 collective-permute-start
  20.2 5.9 %collective-permute-done = bf16[128,128]{1,0:T(8,128)(2,1)} collective-permute-done((bf16[128,128]{1,0:T(8,128)(2,1)S(1)}, bf16[128,128]{1,0:T(8,128)(2,1)}, u32[]{:S(2)}, u32[]{:S(2)}) %collective-permute-start) | collective-permute-done | bytes 32800 | tf_op jit(solution)/shard_map/ppermute | solution.py:14
  26.1 1.9 collective-permute-start.1
  27.9 3.9 collective-permute-start.10
  31.8 2.9 collective-permute-start.9
  34.8 2.9 collective-permute-start.7
  37.7 2.9 collective-permute-start.3
  40.6 1.2 copy.27
  42.6 2.9 collective-permute-start.2
  46.3 1.3 collective-permute-start.6
  47.6 2.9 collective-permute-done.2
  50.5 1.3 collective-permute-start.4
  51.8 3.0 collective-permute-start.5
  54.9 1.3 collective-permute-start.11
  56.2 3.8 collective-permute-start.8
  62.1 2.1 copy.49
  64.1 1.2 fusion.61
  66.3 47.7 %all_gather.9 = bf16[2048,128]{1,0:T(8,128)(2,1)S(1)} all-gather(bf16[64,128]{1,0:T(8,128)(2,1)S(1)} %convolution_convert_fusion.8), channel_id=1, replica_groups=mesh['sub'=32,'col'=8] {'sub'}, dimensions={0}, use_global_device_ids=true | all-gather | bytes 540672 | tf_op jit(solution)/shard_map/all_gather | solution.py:84
  115.7 33.5 %reduce-scatter.10.cloned.1.call-done = bf16[64,128]{1,0:T(8,128)(2,1)} async-done(((bf16[512,128]{1,0:T(8,128)(2,1)}), bf16[64,128]{1,0:T(8,128)(2,1)}) %reduce-scatter.10.cloned.1.call-update) | async-done | bytes 16400
  149.2 1.3 fusion.27
  150.5 6.9 %fusion.51 = bf16[1536,128]{0,1:T(8,128)(2,1)S(1)} fusion(bf16[1,1,1536,1536]{3,2,1,0:T(8,128)(2,1)} %param.11, bf16[1536,128]{0,1:T(8,128)(2,1)S(1)} %fusion.27, bf16[1,1,1536,1536]{3,2,1,0:T(8,128)(2,1)} %param.10), kind=kOutput, calls=%fused_computation.30 | convolution fusion | flops 1208942592 | bytes 10223616 | tf_op jit(solution)/shard_map/dot_general | solution.py:65
  158.2 1.1 copy.50
  159.7 3.5 collective-permute-start.12
  163.2 4.4 %collective-permute-done.12 = bf16[128,128]{1,0:T(8,128)(2,1)S(1)} collective-permute-done((bf16[128,128]{1,0:T(8,128)(2,1)S(1)}, bf16[128,128]{1,0:T(8,128)(2,1)S(1)}, u32[]{:S(2)}, u32[]{:S(2)}) %collective-permute-start.12) | collective-permute-done | bytes 32800 | tf_op jit(solution)/shard_map/ppermute | solution.py:14
  167.6 1.3 collective-permute-start.13
  168.9 3.1 collective-permute-start.22
  172.0 3.3 collective-permute-start.21
  175.3 3.3 collective-permute-start.19
  178.6 2.6 collective-permute-start.15
  181.2 2.6 collective-permute-start.14
  183.8 2.9 collective-permute-done.15
  186.6 1.3 collective-permute-start.18
  187.9 1.1 collective-permute-done.14
  189.1 1.3 collective-permute-start.16
  190.4 3.0 collective-permute-start.17
  193.4 1.3 collective-permute-start.23
  194.7 3.8 collective-permute-start.20
  200.4 2.1 copy.51
  202.5 1.2 fusion.62
  204.7 47.6 %all_gather.10 = bf16[2048,128]{1,0:T(8,128)(2,1)S(1)} all-gather(bf16[64,128]{1,0:T(8,128)(2,1)S(1)} %convolution_convert_fusion.7), channel_id=1, replica_groups=mesh['sub'=32,'col'=8] {'sub'}, dimensions={0}, use_global_device_ids=true | all-gather | bytes 540672 | tf_op jit(solution)/shard_map/all_gather | solution.py:84
  254.1 31.7 %reduce-scatter.12.cloned.1.call-done = bf16[64,128]{1,0:T(8,128)(2,1)} async-done(((bf16[512,128]{1,0:T(8,128)(2,1)}), bf16[64,128]{1,0:T(8,128)(2,1)}) %reduce-scatter.12.cloned.1.call-update) | async-done | bytes 16400
  285.8 1.3 fusion.28
  287.1 6.9 %fusion.48 = bf16[1536,128]{0,1:T(8,128)(2,1)S(1)} fusion(bf16[1,1,1536,1536]{3,2,1,0:T(8,128)(2,1)} %param.11, bf16[1536,128]{0,1:T(8,128)(2,1)S(1)} %fusion.28, bf16[1,1,1536,1536]{3,2,1,0:T(8,128)(2,1)} %param.10), kind=kOutput, calls=%fused_computation.29 | convolution fusion | flops 1208942592 | bytes 10223616 | tf_op jit(solution)/shard_map/dot_general | solution.py:65
  296.4 3.5 collective-permute-start.24
  299.8 4.5 %collective-permute-done.24 = bf16[128,128]{1,0:T(8,128)(2,1)S(1)} collective-permute-done((bf16[128,128]{1,0:T(8,128)(2,1)S(1)}, bf16[128,128]{1,0:T(8,128)(2,1)S(1)}, u32[]{:S(2)}, u32[]{:S(2)}) %collective-permute-start.24) | collective-permute-done | bytes 32800 | tf_op jit(solution)/shard_map/ppermute | solution.py:14
  304.3 1.3 collective-permute-start.25
  305.6 3.0 collective-permute-start.34
  308.6 3.4 collective-permute-start.33
  312.0 3.2 collective-permute-start.31
  315.2 2.6 collective-permute-start.27
  317.8 2.5 collective-permute-start.26
  320.3 3.0 collective-permute-done.27
  323.3 1.3 collective-permute-start.30
  324.6 1.2 collective-permute-done.26
  325.7 1.3 collective-permute-start.28
  327.1 3.0 collective-permute-start.29
  330.1 1.3 collective-permute-start.35
  331.4 3.8 collective-permute-start.32
  337.1 2.1 copy.53
  339.2 1.3 fusion.63
  340.7 47.7 %all_gather.11 = bf16[2048,128]{1,0:T(8,128)(2,1)S(1)} all-gather(bf16[64,128]{1,0:T(8,128)(2,1)S(1)} %convolution_convert_fusion.6), channel_id=1, replica_groups=mesh['sub'=32,'col'=8] {'sub'}, dimensions={0}, use_global_device_ids=true | all-gather | bytes 540672 | tf_op jit(solution)/shard_map/all_gather | solution.py:84
  390.9 31.0 %reduce-scatter.14.cloned.1.call-done = bf16[64,128]{1,0:T(8,128)(2,1)} async-done(((bf16[512,128]{1,0:T(8,128)(2,1)}), bf16[64,128]{1,0:T(8,128)(2,1)}) %reduce-scatter.14.cloned.1.call-update) | async-done | bytes 16400
  (100 shorter events, 21.6 us)
Async XLA Ops:
  7.2 106.8 %copy-start = (bf16[512,2048]{1,0:T(8,128)(2,1)S(1)}, bf16[512,2048]{1,0:T(8,128)(2,1)}, u32[]{:S(2)}) copy-start(bf16[512,2048]{1,0:T(8,128)(2,1)} %param.15) | copy-start | bytes 6291460
  7.2 142.0 %reduce-scatter.10.cloned.1.call-start = ((), (), s32[]{:S(2)}) async-start(), calls=%async_computation.3 | async-start | bytes 147456
  8.5 7.3 %copy-start.5 = (s32[1,1,8,128]{3,2,1,0:T(8,128)S(1)}, s32[1,1,8,128]{3,2,1,0:T(8,128)}, u32[]{:S(2)}) copy-start(s32[1,1,8,128]{3,2,1,0:T(8,128)} %param.12) | copy-start | bytes 12292
  8.6 33.2 %copy-start.4 = (bf16[1,1,1536]{2,1,0:T(2,128)(2,1)S(1)}, bf16[1,1,1536]{2,1,0:T(2,128)(2,1)}, u32[]{:S(2)}) copy-start(bf16[1,1,1536]{2,1,0:T(2,128)(2,1)} %param.14) | copy-start | bytes 9220
  16.3 9.7 %collective-permute-start = (bf16[128,128]{1,0:T(8,128)(2,1)S(1)}, bf16[128,128]{1,0:T(8,128)(2,1)}, u32[]{:S(2)}, u32[]{:S(2)}) collective-permute-start(bf16[128,128]{1,0:T(8,128)(2,1)S(1)} %get-tuple-element.29), channel_id=1, source_target_pairs={{0,8},{8,16},{16,24},{24,32},{32,40},{40,48},{48,56},{56,64},{64,7... | collective-permute-start | bytes 98312 | tf_op jit(solution)/shard_map/ppermute | solution.py:14
  26.1 16.5 %collective-permute-start.1 = (bf16[128,128]{1,0:T(8,128)(2,1)}, bf16[128,128]{1,0:T(8,128)(2,1)}, u32[]{:S(2)}, u32[]{:S(2)}) collective-permute-start(bf16[128,128]{1,0:T(8,128)(2,1)} %collective-permute-done), channel_id=1, source_target_pairs={{0,1},{1,2},{2,3},{3,4},{4,5},{5,6},{6,7},{8,9},{9,10},{10,11},{11... | collective-permute-start | bytes 98312 | tf_op jit(solution)/shard_map/ppermute | solution.py:14
  27.9 23.9 %collective-permute-start.10 = (bf16[128,128]{1,0:T(8,128)(2,1)S(1)}, bf16[128,128]{1,0:T(8,128)(2,1)}, u32[]{:S(2)}, u32[]{:S(2)}) collective-permute-start(bf16[128,128]{1,0:T(8,128)(2,1)S(1)} %get-tuple-element.22), channel_id=1, source_target_pairs={{8,0},{16,8},{24,16},{32,24},{40,32},{48,40},{56,48},{64,56},{72,6... | collective-permute-start | bytes 98312 | tf_op jit(solution)/shard_map/ppermute | solution.py:14
  31.8 29.2 %collective-permute-start.9 = (bf16[128,128]{1,0:T(8,128)(2,1)S(1)}, bf16[128,128]{1,0:T(8,128)(2,1)S(1)}, u32[]{:S(2)}, u32[]{:S(2)}) collective-permute-start(bf16[128,128]{1,0:T(8,128)(2,1)S(1)} %get-tuple-element.23), channel_id=1, source_target_pairs={{8,0},{16,8},{24,16},{32,24},{40,32},{48,40},{56,48},{64,56},{72,6... | collective-permute-start | bytes 98312 | tf_op jit(solution)/shard_map/ppermute | solution.py:14
  34.8 20.1 %collective-permute-start.7 = (bf16[128,128]{1,0:T(8,128)(2,1)S(1)}, bf16[128,128]{1,0:T(8,128)(2,1)}, u32[]{:S(2)}, u32[]{:S(2)}) collective-permute-start(bf16[128,128]{1,0:T(8,128)(2,1)S(1)} %get-tuple-element.24), channel_id=1, source_target_pairs={{8,0},{16,8},{24,16},{32,24},{40,32},{48,40},{56,48},{64,56},{72,6... | collective-permute-start | bytes 98312 | tf_op jit(solution)/shard_map/ppermute | solution.py:14
  37.7 8.6 %collective-permute-start.3 = (bf16[128,128]{1,0:T(8,128)(2,1)S(1)}, bf16[128,128]{1,0:T(8,128)(2,1)}, u32[]{:S(2)}, u32[]{:S(2)}) collective-permute-start(bf16[128,128]{1,0:T(8,128)(2,1)S(1)} %get-tuple-element.27), channel_id=1, source_target_pairs={{0,8},{8,16},{16,24},{24,32},{32,40},{40,48},{48,56},{56,64},{64,7... | collective-permute-start | bytes 98312 | tf_op jit(solution)/shard_map/ppermute | solution.py:14
  42.6 7.9 %collective-permute-start.2 = (bf16[128,128]{1,0:T(8,128)(2,1)S(1)}, bf16[128,128]{1,0:T(8,128)(2,1)S(1)}, u32[]{:S(2)}, u32[]{:S(2)}) collective-permute-start(bf16[128,128]{1,0:T(8,128)(2,1)S(1)} %get-tuple-element.28), channel_id=1, source_target_pairs={{0,8},{8,16},{16,24},{24,32},{32,40},{40,48},{48,56},{56,64},{64,7... | collective-permute-start | bytes 98312 | tf_op jit(solution)/shard_map/ppermute | solution.py:14
  46.3 13.7 %collective-permute-start.6 = (bf16[128,128]{1,0:T(8,128)(2,1)S(1)}, bf16[128,128]{1,0:T(8,128)(2,1)S(1)}, u32[]{:S(2)}, u32[]{:S(2)}) collective-permute-start(bf16[128,128]{1,0:T(8,128)(2,1)S(1)} %get-tuple-element.25), channel_id=1, source_target_pairs={{1,0},{2,1},{3,2},{4,3},{5,4},{6,5},{7,6},{9,8},{10,9},{11,10},{12... | collective-permute-start | bytes 98312 | tf_op jit(solution)/shard_map/ppermute | solution.py:14
  50.5 5.7 %collective-permute-start.4 = (bf16[128,128]{1,0:T(8,128)(2,1)}, bf16[128,128]{1,0:T(8,128)(2,1)S(1)}, u32[]{:S(2)}, u32[]{:S(2)}) collective-permute-start(bf16[128,128]{1,0:T(8,128)(2,1)} %collective-permute-done.3), channel_id=1, source_target_pairs={{1,0},{2,1},{3,2},{4,3},{5,4},{6,5},{7,6},{9,8},{10,9},{11,10},{12... | collective-permute-start | bytes 98312 | tf_op jit(solution)/shard_map/ppermute | solution.py:14
  51.8 8.2 %collective-permute-start.5 = (bf16[128,128]{1,0:T(8,128)(2,1)S(1)}, bf16[128,128]{1,0:T(8,128)(2,1)S(1)}, u32[]{:S(2)}, u32[]{:S(2)}) collective-permute-start(bf16[128,128]{1,0:T(8,128)(2,1)S(1)} %get-tuple-element.26), channel_id=1, source_target_pairs={{0,1},{1,2},{2,3},{3,4},{4,5},{5,6},{6,7},{8,9},{9,10},{10,11},{11... | collective-permute-start | bytes 98312 | tf_op jit(solution)/shard_map/ppermute | solution.py:14
  54.9 6.2 %collective-permute-start.11 = (bf16[128,128]{1,0:T(8,128)(2,1)}, bf16[128,128]{1,0:T(8,128)(2,1)S(1)}, u32[]{:S(2)}, u32[]{:S(2)}) collective-permute-start(bf16[128,128]{1,0:T(8,128)(2,1)} %collective-permute-done.10), channel_id=1, source_target_pairs={{1,0},{2,1},{3,2},{4,3},{5,4},{6,5},{7,6},{9,8},{10,9},{11,10},{12... | collective-permute-start | bytes 98312 | tf_op jit(solution)/shard_map/ppermute | solution.py:14
  56.2 4.8 %collective-permute-start.8 = (bf16[128,128]{1,0:T(8,128)(2,1)}, bf16[128,128]{1,0:T(8,128)(2,1)S(1)}, u32[]{:S(2)}, u32[]{:S(2)}) collective-permute-start(bf16[128,128]{1,0:T(8,128)(2,1)} %collective-permute-done.7), channel_id=1, source_target_pairs={{0,1},{1,2},{2,3},{3,4},{4,5},{5,6},{6,7},{8,9},{9,10},{10,11},{11... | collective-permute-start | bytes 98312 | tf_op jit(solution)/shard_map/ppermute | solution.py:14
  65.3 0.7 copy-start.2
  115.6 170.2 %reduce-scatter.12.cloned.1.call-start = ((), (), s32[]{:S(2)}) async-start(), calls=%async_computation.4 | async-start | bytes 147456
  159.7 7.9 %collective-permute-start.12 = (bf16[128,128]{1,0:T(8,128)(2,1)S(1)}, bf16[128,128]{1,0:T(8,128)(2,1)S(1)}, u32[]{:S(2)}, u32[]{:S(2)}) collective-permute-start(bf16[128,128]{1,0:T(8,128)(2,1)S(1)} %get-tuple-element.21), channel_id=1, source_target_pairs={{0,8},{8,16},{16,24},{24,32},{32,40},{40,48},{48,56},{56,64},{64,7... | collective-permute-start | bytes 98312 | tf_op jit(solution)/shard_map/ppermute | solution.py:14
  167.6 13.5 %collective-permute-start.13 = (bf16[128,128]{1,0:T(8,128)(2,1)S(1)}, bf16[128,128]{1,0:T(8,128)(2,1)S(1)}, u32[]{:S(2)}, u32[]{:S(2)}) collective-permute-start(bf16[128,128]{1,0:T(8,128)(2,1)S(1)} %collective-permute-done.12), channel_id=1, source_target_pairs={{0,1},{1,2},{2,3},{3,4},{4,5},{5,6},{6,7},{8,9},{9,10},{10,11},{11... | collective-permute-start | bytes 98312 | tf_op jit(solution)/shard_map/ppermute | solution.py:14
  168.9 21.5 %collective-permute-start.22 = (bf16[128,128]{1,0:T(8,128)(2,1)S(1)}, bf16[128,128]{1,0:T(8,128)(2,1)S(1)}, u32[]{:S(2)}, u32[]{:S(2)}) collective-permute-start(bf16[128,128]{1,0:T(8,128)(2,1)S(1)} %get-tuple-element.14), channel_id=1, source_target_pairs={{8,0},{16,8},{24,16},{32,24},{40,32},{48,40},{56,48},{64,56},{72,6... | collective-permute-start | bytes 98312 | tf_op jit(solution)/shard_map/ppermute | solution.py:14
  172.0 27.4 %collective-permute-start.21 = (bf16[128,128]{1,0:T(8,128)(2,1)S(1)}, bf16[128,128]{1,0:T(8,128)(2,1)S(1)}, u32[]{:S(2)}, u32[]{:S(2)}) collective-permute-start(bf16[128,128]{1,0:T(8,128)(2,1)S(1)} %get-tuple-element.15), channel_id=1, source_target_pairs={{8,0},{16,8},{24,16},{32,24},{40,32},{48,40},{56,48},{64,56},{72,6... | collective-permute-start | bytes 98312 | tf_op jit(solution)/shard_map/ppermute | solution.py:14
  175.3 18.1 %collective-permute-start.19 = (bf16[128,128]{1,0:T(8,128)(2,1)S(1)}, bf16[128,128]{1,0:T(8,128)(2,1)S(1)}, u32[]{:S(2)}, u32[]{:S(2)}) collective-permute-start(bf16[128,128]{1,0:T(8,128)(2,1)S(1)} %get-tuple-element.16), channel_id=1, source_target_pairs={{8,0},{16,8},{24,16},{32,24},{40,32},{48,40},{56,48},{64,56},{72,6... | collective-permute-start | bytes 98312 | tf_op jit(solution)/shard_map/ppermute | solution.py:14
  178.6 8.1 %collective-permute-start.15 = (bf16[128,128]{1,0:T(8,128)(2,1)S(1)}, bf16[128,128]{1,0:T(8,128)(2,1)S(1)}, u32[]{:S(2)}, u32[]{:S(2)}) collective-permute-start(bf16[128,128]{1,0:T(8,128)(2,1)S(1)} %get-tuple-element.19), channel_id=1, source_target_pairs={{0,8},{8,16},{16,24},{24,32},{32,40},{40,48},{48,56},{56,64},{64,7... | collective-permute-start | bytes 98312 | tf_op jit(solution)/shard_map/ppermute | solution.py:14
  181.2 7.9 %collective-permute-start.14 = (bf16[128,128]{1,0:T(8,128)(2,1)S(1)}, bf16[128,128]{1,0:T(8,128)(2,1)S(1)}, u32[]{:S(2)}, u32[]{:S(2)}) collective-permute-start(bf16[128,128]{1,0:T(8,128)(2,1)S(1)} %get-tuple-element.20), channel_id=1, source_target_pairs={{0,8},{8,16},{16,24},{24,32},{32,40},{40,48},{48,56},{56,64},{64,7... | collective-permute-start | bytes 98312 | tf_op jit(solution)/shard_map/ppermute | solution.py:14
  186.6 11.9 %collective-permute-start.18 = (bf16[128,128]{1,0:T(8,128)(2,1)S(1)}, bf16[128,128]{1,0:T(8,128)(2,1)S(1)}, u32[]{:S(2)}, u32[]{:S(2)}) collective-permute-start(bf16[128,128]{1,0:T(8,128)(2,1)S(1)} %get-tuple-element.17), channel_id=1, source_target_pairs={{1,0},{2,1},{3,2},{4,3},{5,4},{6,5},{7,6},{9,8},{10,9},{11,10},{12... | collective-permute-start | bytes 98312 | tf_op jit(solution)/shard_map/ppermute | solution.py:14
  189.1 5.7 %collective-permute-start.16 = (bf16[128,128]{1,0:T(8,128)(2,1)S(1)}, bf16[128,128]{1,0:T(8,128)(2,1)S(1)}, u32[]{:S(2)}, u32[]{:S(2)}) collective-permute-start(bf16[128,128]{1,0:T(8,128)(2,1)S(1)} %collective-permute-done.15), channel_id=1, source_target_pairs={{1,0},{2,1},{3,2},{4,3},{5,4},{6,5},{7,6},{9,8},{10,9},{11,10},{12... | collective-permute-start | bytes 98312 | tf_op jit(solution)/shard_map/ppermute | solution.py:14
  190.4 8.2 %collective-permute-start.17 = (bf16[128,128]{1,0:T(8,128)(2,1)S(1)}, bf16[128,128]{1,0:T(8,128)(2,1)S(1)}, u32[]{:S(2)}, u32[]{:S(2)}) collective-permute-start(bf16[128,128]{1,0:T(8,128)(2,1)S(1)} %get-tuple-element.18), channel_id=1, source_target_pairs={{0,1},{1,2},{2,3},{3,4},{4,5},{5,6},{6,7},{8,9},{9,10},{10,11},{11... | collective-permute-start | bytes 98312 | tf_op jit(solution)/shard_map/ppermute | solution.py:14
  193.4 6.0 %collective-permute-start.23 = (bf16[128,128]{1,0:T(8,128)(2,1)S(1)}, bf16[128,128]{1,0:T(8,128)(2,1)S(1)}, u32[]{:S(2)}, u32[]{:S(2)}) collective-permute-start(bf16[128,128]{1,0:T(8,128)(2,1)S(1)} %collective-permute-done.22), channel_id=1, source_target_pairs={{1,0},{2,1},{3,2},{4,3},{5,4},{6,5},{7,6},{9,8},{10,9},{11,10},{12... | collective-permute-start | bytes 98312 | tf_op jit(solution)/shard_map/ppermute | solution.py:14
  194.7 4.6 %collective-permute-start.20 = (bf16[128,128]{1,0:T(8,128)(2,1)S(1)}, bf16[128,128]{1,0:T(8,128)(2,1)S(1)}, u32[]{:S(2)}, u32[]{:S(2)}) collective-permute-start(bf16[128,128]{1,0:T(8,128)(2,1)S(1)} %collective-permute-done.19), channel_id=1, source_target_pairs={{0,1},{1,2},{2,3},{3,4},{4,5},{5,6},{6,7},{8,9},{9,10},{10,11},{11... | collective-permute-start | bytes 98312 | tf_op jit(solution)/shard_map/ppermute | solution.py:14
  203.7 0.7 copy-start.3
  253.9 168.0 %reduce-scatter.14.cloned.1.call-start = ((), (), s32[]{:S(2)}) async-start(), calls=%async_computation.5 | async-start | bytes 147456
  294.1 43.1 %copy-start.1 = (bf16[1536,128]{0,1:T(8,128)(2,1)}, bf16[1536,128]{0,1:T(8,128)(2,1)S(1)}, u32[]{:S(2)}) copy-start(bf16[1536,128]{0,1:T(8,128)(2,1)S(1)} %fusion.48) | copy-start | bytes 1179652
  296.4 7.9 %collective-permute-start.24 = (bf16[128,128]{1,0:T(8,128)(2,1)S(1)}, bf16[128,128]{1,0:T(8,128)(2,1)S(1)}, u32[]{:S(2)}, u32[]{:S(2)}) collective-permute-start(bf16[128,128]{1,0:T(8,128)(2,1)S(1)} %get-tuple-element.13), channel_id=1, source_target_pairs={{0,8},{8,16},{16,24},{24,32},{32,40},{40,48},{48,56},{56,64},{64,7... | collective-permute-start | bytes 98312 | tf_op jit(solution)/shard_map/ppermute | solution.py:14
  304.3 13.5 %collective-permute-start.25 = (bf16[128,128]{1,0:T(8,128)(2,1)S(1)}, bf16[128,128]{1,0:T(8,128)(2,1)S(1)}, u32[]{:S(2)}, u32[]{:S(2)}) collective-permute-start(bf16[128,128]{1,0:T(8,128)(2,1)S(1)} %collective-permute-done.24), channel_id=1, source_target_pairs={{0,1},{1,2},{2,3},{3,4},{4,5},{5,6},{6,7},{8,9},{9,10},{10,11},{11... | collective-permute-start | bytes 98312 | tf_op jit(solution)/shard_map/ppermute | solution.py:14
  305.6 21.5 %collective-permute-start.34 = (bf16[128,128]{1,0:T(8,128)(2,1)S(1)}, bf16[128,128]{1,0:T(8,128)(2,1)S(1)}, u32[]{:S(2)}, u32[]{:S(2)}) collective-permute-start(bf16[128,128]{1,0:T(8,128)(2,1)S(1)} %get-tuple-element.6), channel_id=1, source_target_pairs={{8,0},{16,8},{24,16},{32,24},{40,32},{48,40},{56,48},{64,56},{72,6... | collective-permute-start | bytes 98312 | tf_op jit(solution)/shard_map/ppermute | solution.py:14
  308.6 27.5 %collective-permute-start.33 = (bf16[128,128]{1,0:T(8,128)(2,1)S(1)}, bf16[128,128]{1,0:T(8,128)(2,1)S(1)}, u32[]{:S(2)}, u32[]{:S(2)}) collective-permute-start(bf16[128,128]{1,0:T(8,128)(2,1)S(1)} %get-tuple-element.7), channel_id=1, source_target_pairs={{8,0},{16,8},{24,16},{32,24},{40,32},{48,40},{56,48},{64,56},{72,6... | collective-permute-start | bytes 98312 | tf_op jit(solution)/shard_map/ppermute | solution.py:14
  312.0 18.1 %collective-permute-start.31 = (bf16[128,128]{1,0:T(8,128)(2,1)S(1)}, bf16[128,128]{1,0:T(8,128)(2,1)S(1)}, u32[]{:S(2)}, u32[]{:S(2)}) collective-permute-start(bf16[128,128]{1,0:T(8,128)(2,1)S(1)} %get-tuple-element.8), channel_id=1, source_target_pairs={{8,0},{16,8},{24,16},{32,24},{40,32},{48,40},{56,48},{64,56},{72,6... | collective-permute-start | bytes 98312 | tf_op jit(solution)/shard_map/ppermute | solution.py:14
  315.2 8.1 %collective-permute-start.27 = (bf16[128,128]{1,0:T(8,128)(2,1)S(1)}, bf16[128,128]{1,0:T(8,128)(2,1)S(1)}, u32[]{:S(2)}, u32[]{:S(2)}) collective-permute-start(bf16[128,128]{1,0:T(8,128)(2,1)S(1)} %get-tuple-element.11), channel_id=1, source_target_pairs={{0,8},{8,16},{16,24},{24,32},{32,40},{40,48},{48,56},{56,64},{64,7... | collective-permute-start | bytes 98312 | tf_op jit(solution)/shard_map/ppermute | solution.py:14
  317.8 7.9 %collective-permute-start.26 = (bf16[128,128]{1,0:T(8,128)(2,1)S(1)}, bf16[128,128]{1,0:T(8,128)(2,1)S(1)}, u32[]{:S(2)}, u32[]{:S(2)}) collective-permute-start(bf16[128,128]{1,0:T(8,128)(2,1)S(1)} %get-tuple-element.12), channel_id=1, source_target_pairs={{0,8},{8,16},{16,24},{24,32},{32,40},{40,48},{48,56},{56,64},{64,7... | collective-permute-start | bytes 98312 | tf_op jit(solution)/shard_map/ppermute | solution.py:14
  323.3 11.9 %collective-permute-start.30 = (bf16[128,128]{1,0:T(8,128)(2,1)S(1)}, bf16[128,128]{1,0:T(8,128)(2,1)S(1)}, u32[]{:S(2)}, u32[]{:S(2)}) collective-permute-start(bf16[128,128]{1,0:T(8,128)(2,1)S(1)} %get-tuple-element.9), channel_id=1, source_target_pairs={{1,0},{2,1},{3,2},{4,3},{5,4},{6,5},{7,6},{9,8},{10,9},{11,10},{12... | collective-permute-start | bytes 98312 | tf_op jit(solution)/shard_map/ppermute | solution.py:14
  325.7 5.7 %collective-permute-start.28 = (bf16[128,128]{1,0:T(8,128)(2,1)S(1)}, bf16[128,128]{1,0:T(8,128)(2,1)S(1)}, u32[]{:S(2)}, u32[]{:S(2)}) collective-permute-start(bf16[128,128]{1,0:T(8,128)(2,1)S(1)} %collective-permute-done.27), channel_id=1, source_target_pairs={{1,0},{2,1},{3,2},{4,3},{5,4},{6,5},{7,6},{9,8},{10,9},{11,10},{12... | collective-permute-start | bytes 98312 | tf_op jit(solution)/shard_map/ppermute | solution.py:14
  327.1 8.2 %collective-permute-start.29 = (bf16[128,128]{1,0:T(8,128)(2,1)S(1)}, bf16[128,128]{1,0:T(8,128)(2,1)S(1)}, u32[]{:S(2)}, u32[]{:S(2)}) collective-permute-start(bf16[128,128]{1,0:T(8,128)(2,1)S(1)} %get-tuple-element.10), channel_id=1, source_target_pairs={{0,1},{1,2},{2,3},{3,4},{4,5},{5,6},{6,7},{8,9},{9,10},{10,11},{11... | collective-permute-start | bytes 98312 | tf_op jit(solution)/shard_map/ppermute | solution.py:14
  330.1 6.0 %collective-permute-start.35 = (bf16[128,128]{1,0:T(8,128)(2,1)S(1)}, bf16[128,128]{1,0:T(8,128)(2,1)S(1)}, u32[]{:S(2)}, u32[]{:S(2)}) collective-permute-start(bf16[128,128]{1,0:T(8,128)(2,1)S(1)} %collective-permute-done.34), channel_id=1, source_target_pairs={{1,0},{2,1},{3,2},{4,3},{5,4},{6,5},{7,6},{9,8},{10,9},{11,10},{12... | collective-permute-start | bytes 98312 | tf_op jit(solution)/shard_map/ppermute | solution.py:14
  331.4 4.6 %collective-permute-start.32 = (bf16[128,128]{1,0:T(8,128)(2,1)S(1)}, bf16[128,128]{1,0:T(8,128)(2,1)S(1)}, u32[]{:S(2)}, u32[]{:S(2)}) collective-permute-start(bf16[128,128]{1,0:T(8,128)(2,1)S(1)} %collective-permute-done.31), channel_id=1, source_target_pairs={{0,1},{1,2},{2,3},{3,4},{4,5},{5,6},{6,7},{8,9},{9,10},{10,11},{11... | collective-permute-start | bytes 98312 | tf_op jit(solution)/shard_map/ppermute | solution.py:14
Sparse Core Ops, SparseCore 0:
  115.8 33.4 reduce-scatter.9
  254.0 31.7 reduce-scatter.11
  390.1 31.7 reduce-scatter.13
where the time goes:
time: 432 us; the launch traced here: 430 us
  blocking collectives  143 us (33%)
  waiting for transfers between devices  125 us (29%)
  starting transfers between devices  92.6 us (21%)
  matrix products  31.9 us (7%)
  local copies, waits for them, and re-layouts  19.3 us (4%)
  between operations  14.6 us (3%)
  other arithmetic  4.39 us (1%)
    all_gather x3, blocking collectives, local(): lax.all_gather(coarse_rhs, 'sub', axis=0, tiled=True)  143 us
    unnamed x6, waiting for transfers between devices  96.2 us
    ppermute x36, starting transfers between devices, from_behind(): return lax.ppermute(value, axis, pairs)  92.3 us
    ppermute x36, waiting for transfers between devices, from_behind(): return lax.ppermute(value, axis, pairs)  28.5 us
    dot_general x3, matrix products, local(): jnp.dot(inverse, mixed_trace, preferred_element_type=jnp.float32)  21 us
    unnamed x40, local copies, waits for them, and re-layouts  9.05 us
  transfers between devices with their start and end apart: 39, of which 14 were waited for; matrix products, arithmetic and copies ran while one was open for 1% of the time, Pallas kernels for 0%

commit v1 on v0

--- a/solution.py
+++ b/solution.py
@@ -6,6 +6,11 @@
 MODES = 64
 ITERS = 3
 DIRECTIONS = ((-1, -1), (-1, 0), (-1, 1), (0, -1), (0, 1), (1, -1), (1, 0), (1, 1))
+
+
+def gather_from_all(value, axis, dim):
+    copies = jnp.concatenate([value] * lax.axis_size(axis), axis=dim)
+    return lax.all_to_all(copies, axis, dim, dim, tiled=True)
 
 
 def from_behind(value, axis, by):
@@ -81,7 +86,7 @@
         )
         partial_value = jnp.dot(
             coarse_inverse,
-            lax.all_gather(coarse_rhs, "sub", axis=0, tiled=True),
+            gather_from_all(coarse_rhs, "sub", 0),
             preferred_element_type=jnp.float32,
         )
         coarse_out = lax.psum_scatter(

time: 432 us -> 352 us (0.81)
  blocking collectives: 143 us -> 61.5 us
    all_gather x3 -> x0, blocking collectives: 143 us -> none  [local(): lax.all_gather(coarse_rhs, 'sub', axis=0, tiled=True)]
    all_to_all x0 -> x3, blocking collectives: none -> 61.5 us  [gather_from_all(): return lax.all_to_all(copies, axis, dim, dim, tiled=True)]
    unnamed x40 -> x130, local copies, waits for them, and re-layouts: 9.05 us -> 8.57 us
where the time goes in v1:
time: 352 us; the launch traced here: 350 us
  waiting for transfers between devices  126 us (36%)
  starting transfers between devices  92.8 us (26%)
  blocking collectives  61.5 us (17%)
  matrix products  31.8 us (9%)
  local copies, waits for them, and re-layouts  18.9 us (5%)
  between operations  14.9 us (4%)
  other arithmetic  4.39 us (1%)
    unnamed x6, waiting for transfers between devices  97.6 us
    ppermute x36, starting transfers between devices, from_behind(): return lax.ppermute(value, axis, pairs)  92.5 us
    all_to_all x3, blocking collectives, gather_from_all(): return lax.all_to_all(copies, axis, dim, dim, tiled=True)  61.5 us
    ppermute x36, waiting for transfers between devices, from_behind(): return lax.ppermute(value, axis, pairs)  28.3 us
    dot_general x3, matrix products, local(): jnp.dot(inverse, mixed_trace, preferred_element_type=jnp.float32)  21 us
    unnamed x130, local copies, waits for them, and re-layouts  8.57 us
  transfers between devices with their start and end apart: 39, of which 14 were waited for; matrix products, arithmetic and copies ran while one was open for 1% of the time, Pallas kernels for 0%

profile of v1, /device:TPU:2, one launch (start us, length us, event | category | flops | bytes accessed | tf_op | source)
XLA Modules:
  0.0 350.2 jit_solution(17364207616822793384)
XLA Ops:
  7.2 1.3 copy.26
  8.6 7.1 %fusion.54 = bf16[1536,128]{0,1:T(8,128)(2,1)S(1)} fusion(bf16[1,1,1536,1536]{3,2,1,0:T(8,128)(2,1)} %param.11, bf16[1,1,1536,1536]{3,2,1,0:T(8,128)(2,1)} %param.10, bf16[1,1,1536,128]{3,2,1,0:T(8,128)(2,1)} %param.8, bf16[1,1,1536,128]{2,3,1,0:T(8,128)(2,1)S(1)} %copy.26), kind=kOutput, calls=%fused_computation.31 | convolution fusion | flops 1208942592 | bytes 10616832 | tf_op jit(solution)/shard_map/dot_general | solution.py:70
  16.3 3.8 %collective-permute-start = (bf16[128,128]{1,0:T(8,128)(2,1)S(1)}, bf16[128,128]{1,0:T(8,128)(2,1)}, u32[]{:S(2)}, u32[]{:S(2)}) collective-permute-start(bf16[128,128]{1,0:T(8,128)(2,1)S(1)} %get-tuple-element.29), channel_id=1, source_target_pairs={{0,8},{8,16},{16,24},{24,32},{32,40},{40,48},{48,56},{56,64},{64,7... | collective-permute-start | bytes 98312 | tf_op jit(solution)/shard_map/ppermute | solution.py:19
  20.2 5.9 %collective-permute-done = bf16[128,128]{1,0:T(8,128)(2,1)} collective-permute-done((bf16[128,128]{1,0:T(8,128)(2,1)S(1)}, bf16[128,128]{1,0:T(8,128)(2,1)}, u32[]{:S(2)}, u32[]{:S(2)}) %collective-permute-start) | collective-permute-done | bytes 32800 | tf_op jit(solution)/shard_map/ppermute | solution.py:19
  26.1 1.9 collective-permute-start.1
  27.9 3.9 %collective-permute-start.10 = (bf16[128,128]{1,0:T(8,128)(2,1)S(1)}, bf16[128,128]{1,0:T(8,128)(2,1)}, u32[]{:S(2)}, u32[]{:S(2)}) collective-permute-start(bf16[128,128]{1,0:T(8,128)(2,1)S(1)} %get-tuple-element.22), channel_id=1, source_target_pairs={{8,0},{16,8},{24,16},{32,24},{40,32},{48,40},{56,48},{64,56},{72,6... | collective-permute-start | bytes 98312 | tf_op jit(solution)/shard_map/ppermute | solution.py:19
  31.9 2.9 collective-permute-start.9
  34.8 2.9 collective-permute-start.7
  37.7 2.9 collective-permute-start.3
  40.6 1.2 copy.27
  42.6 2.9 collective-permute-start.2
  46.3 1.3 collective-permute-start.6
  47.6 2.9 collective-permute-done.2
  50.5 1.3 collective-permute-start.4
  51.8 3.0 collective-permute-start.5
  54.9 1.3 collective-permute-start.11
  56.2 3.8 %collective-permute-start.8 = (bf16[128,128]{1,0:T(8,128)(2,1)}, bf16[128,128]{1,0:T(8,128)(2,1)S(1)}, u32[]{:S(2)}, u32[]{:S(2)}) collective-permute-start(bf16[128,128]{1,0:T(8,128)(2,1)} %collective-permute-done.7), channel_id=1, source_target_pairs={{0,1},{1,2},{2,3},{3,4},{4,5},{5,6},{6,7},{8,9},{9,10},{10,11},{11... | collective-permute-start | bytes 98312 | tf_op jit(solution)/shard_map/ppermute | solution.py:19
  62.1 2.1 copy.49
  64.2 1.2 fusion.61
  66.1 20.7 %all_to_all.36 = bf16[32,64,128]{2,1,0:T(8,128)(2,1)S(1)} all-to-all(bf16[32,64,128]{2,1,0:T(8,128)(2,1)S(1)} %bitcast.237), channel_id=1, replica_groups=mesh['sub'=32,'col'=8] {'sub'}, dimensions={0} | all-to-all | bytes 1048576 | tf_op jit(solution)/shard_map/all_to_all | solution.py:13
  88.5 34.7 %reduce-scatter.10.cloned.1.call-done = bf16[64,128]{1,0:T(8,128)(2,1)} async-done(((bf16[512,128]{1,0:T(8,128)(2,1)}), bf16[64,128]{1,0:T(8,128)(2,1)}) %reduce-scatter.10.cloned.1.call-update) | async-done | bytes 16400
  123.2 1.3 fusion.27
  124.5 6.9 %fusion.51 = bf16[1536,128]{0,1:T(8,128)(2,1)S(1)} fusion(bf16[1,1,1536,1536]{3,2,1,0:T(8,128)(2,1)} %param.11, bf16[1536,128]{0,1:T(8,128)(2,1)S(1)} %fusion.27, bf16[1,1,1536,1536]{3,2,1,0:T(8,128)(2,1)} %param.10), kind=kOutput, calls=%fused_computation.30 | convolution fusion | flops 1208942592 | bytes 10223616 | tf_op jit(solution)/shard_map/dot_general | solution.py:70
  132.2 1.1 copy.50
  133.7 3.5 collective-permute-start.12
  137.1 4.5 %collective-permute-done.12 = bf16[128,128]{1,0:T(8,128)(2,1)S(1)} collective-permute-done((bf16[128,128]{1,0:T(8,128)(2,1)S(1)}, bf16[128,128]{1,0:T(8,128)(2,1)S(1)}, u32[]{:S(2)}, u32[]{:S(2)}) %collective-permute-start.12) | collective-permute-done | bytes 32800 | tf_op jit(solution)/shard_map/ppermute | solution.py:19
  141.6 1.3 collective-permute-start.13
  142.9 3.1 collective-permute-start.22
  146.0 3.3 collective-permute-start.21
  149.3 3.3 collective-permute-start.19
  152.6 2.6 collective-permute-start.15
  155.2 2.5 collective-permute-start.14
  157.7 2.9 collective-permute-done.15
  160.6 1.3 collective-permute-start.18
  161.9 1.2 collective-permute-done.14
  163.1 1.3 collective-permute-start.16
  164.4 3.0 collective-permute-start.17
  167.4 1.3 collective-permute-start.23
  168.8 3.8 %collective-permute-start.20 = (bf16[128,128]{1,0:T(8,128)(2,1)S(1)}, bf16[128,128]{1,0:T(8,128)(2,1)S(1)}, u32[]{:S(2)}, u32[]{:S(2)}) collective-permute-start(bf16[128,128]{1,0:T(8,128)(2,1)S(1)} %collective-permute-done.19), channel_id=1, source_target_pairs={{0,1},{1,2},{2,3},{3,4},{4,5},{5,6},{6,7},{8,9},{9,10},{10,11},{11... | collective-permute-start | bytes 98312 | tf_op jit(solution)/shard_map/ppermute | solution.py:19
  174.4 2.1 copy.51
  176.5 1.2 fusion.62
  178.4 20.4 %all_to_all.37 = bf16[32,64,128]{2,1,0:T(8,128)(2,1)S(1)} all-to-all(bf16[32,64,128]{2,1,0:T(8,128)(2,1)S(1)} %bitcast.238), channel_id=1, replica_groups=mesh['sub'=32,'col'=8] {'sub'}, dimensions={0} | all-to-all | bytes 1048576 | tf_op jit(solution)/shard_map/all_to_all | solution.py:13
  200.6 31.7 %reduce-scatter.12.cloned.1.call-done = bf16[64,128]{1,0:T(8,128)(2,1)} async-done(((bf16[512,128]{1,0:T(8,128)(2,1)}), bf16[64,128]{1,0:T(8,128)(2,1)}) %reduce-scatter.12.cloned.1.call-update) | async-done | bytes 16400
  232.3 1.3 fusion.28
  233.6 6.9 %fusion.48 = bf16[1536,128]{0,1:T(8,128)(2,1)S(1)} fusion(bf16[1,1,1536,1536]{3,2,1,0:T(8,128)(2,1)} %param.11, bf16[1536,128]{0,1:T(8,128)(2,1)S(1)} %fusion.28, bf16[1,1,1536,1536]{3,2,1,0:T(8,128)(2,1)} %param.10), kind=kOutput, calls=%fused_computation.29 | convolution fusion | flops 1208942592 | bytes 10223616 | tf_op jit(solution)/shard_map/dot_general | solution.py:70
  241.4 1.1 copy.52
  242.9 3.6 %collective-permute-start.24 = (bf16[128,128]{1,0:T(8,128)(2,1)S(1)}, bf16[128,128]{1,0:T(8,128)(2,1)S(1)}, u32[]{:S(2)}, u32[]{:S(2)}) collective-permute-start(bf16[128,128]{1,0:T(8,128)(2,1)S(1)} %get-tuple-element.13), channel_id=1, source_target_pairs={{0,8},{8,16},{16,24},{24,32},{32,40},{40,48},{48,56},{56,64},{64,7... | collective-permute-start | bytes 98312 | tf_op jit(solution)/shard_map/ppermute | solution.py:19
  246.4 4.4 %collective-permute-done.24 = bf16[128,128]{1,0:T(8,128)(2,1)S(1)} collective-permute-done((bf16[128,128]{1,0:T(8,128)(2,1)S(1)}, bf16[128,128]{1,0:T(8,128)(2,1)S(1)}, u32[]{:S(2)}, u32[]{:S(2)}) %collective-permute-start.24) | collective-permute-done | bytes 32800 | tf_op jit(solution)/shard_map/ppermute | solution.py:19
  250.8 1.3 collective-permute-start.25
  252.1 3.2 collective-permute-start.34
  255.3 3.2 collective-permute-start.33
  258.5 3.3 collective-permute-start.31
  261.9 2.5 collective-permute-start.27
  264.4 2.6 collective-permute-start.26
  267.0 2.9 collective-permute-done.27
  269.9 1.3 collective-permute-start.30
  272.3 1.3 collective-permute-start.28
  273.6 3.0 collective-permute-start.29
  276.7 1.3 collective-permute-start.35
  278.0 3.8 %collective-permute-start.32 = (bf16[128,128]{1,0:T(8,128)(2,1)S(1)}, bf16[128,128]{1,0:T(8,128)(2,1)S(1)}, u32[]{:S(2)}, u32[]{:S(2)}) collective-permute-start(bf16[128,128]{1,0:T(8,128)(2,1)S(1)} %collective-permute-done.31), channel_id=1, source_target_pairs={{0,1},{1,2},{2,3},{3,4},{4,5},{5,6},{6,7},{8,9},{9,10},{10,11},{11... | collective-permute-start | bytes 98312 | tf_op jit(solution)/shard_map/ppermute | solution.py:19
  283.7 2.1 copy.53
  285.8 1.3 fusion.63
  287.7 20.4 %all_to_all.38 = bf16[32,64,128]{2,1,0:T(8,128)(2,1)S(1)} all-to-all(bf16[32,64,128]{2,1,0:T(8,128)(2,1)S(1)} %bitcast.239), channel_id=1, replica_groups=mesh['sub'=32,'col'=8] {'sub'}, dimensions={0} | all-to-all | bytes 1048576 | tf_op jit(solution)/shard_map/all_to_all | solution.py:13
  310.6 31.1 %reduce-scatter.14.cloned.1.call-done = bf16[64,128]{1,0:T(8,128)(2,1)} async-done(((bf16[512,128]{1,0:T(8,128)(2,1)}), bf16[64,128]{1,0:T(8,128)(2,1)}) %reduce-scatter.14.cloned.1.call-update) | async-done | bytes 16400
  (193 shorter events, 21.1 us)
Async XLA Ops:
  7.2 79.6 %copy-start = (bf16[512,2048]{1,0:T(8,128)(2,1)S(1)}, bf16[512,2048]{1,0:T(8,128)(2,1)}, u32[]{:S(2)}) copy-start(bf16[512,2048]{1,0:T(8,128)(2,1)} %param.15) | copy-start | bytes 6291460
  7.2 116.0 %reduce-scatter.10.cloned.1.call-start = ((), (), s32[]{:S(2)}) async-start(), calls=%async_computation.6 | async-start | bytes 147456
  8.5 7.3 %copy-start.5 = (s32[1,1,8,128]{3,2,1,0:T(8,128)S(1)}, s32[1,1,8,128]{3,2,1,0:T(8,128)}, u32[]{:S(2)}) copy-start(s32[1,1,8,128]{3,2,1,0:T(8,128)} %param.12) | copy-start | bytes 12292
  8.6 33.3 %copy-start.4 = (bf16[1,1,1536]{2,1,0:T(2,128)(2,1)S(1)}, bf16[1,1,1536]{2,1,0:T(2,128)(2,1)}, u32[]{:S(2)}) copy-start(bf16[1,1,1536]{2,1,0:T(2,128)(2,1)} %param.14) | copy-start | bytes 9220
  16.3 9.7 %collective-permute-start = (bf16[128,128]{1,0:T(8,128)(2,1)S(1)}, bf16[128,128]{1,0:T(8,128)(2,1)}, u32[]{:S(2)}, u32[]{:S(2)}) collective-permute-start(bf16[128,128]{1,0:T(8,128)(2,1)S(1)} %get-tuple-element.29), channel_id=1, source_target_pairs={{0,8},{8,16},{16,24},{24,32},{32,40},{40,48},{48,56},{56,64},{64,7... | collective-permute-start | bytes 98312 | tf_op jit(solution)/shard_map/ppermute | solution.py:19
  26.1 16.5 %collective-permute-start.1 = (bf16[128,128]{1,0:T(8,128)(2,1)}, bf16[128,128]{1,0:T(8,128)(2,1)}, u32[]{:S(2)}, u32[]{:S(2)}) collective-permute-start(bf16[128,128]{1,0:T(8,128)(2,1)} %collective-permute-done), channel_id=1, source_target_pairs={{0,1},{1,2},{2,3},{3,4},{4,5},{5,6},{6,7},{8,9},{9,10},{10,11},{11... | collective-permute-start | bytes 98312 | tf_op jit(solution)/shard_map/ppermute | solution.py:19
  27.9 23.9 %collective-permute-start.10 = (bf16[128,128]{1,0:T(8,128)(2,1)S(1)}, bf16[128,128]{1,0:T(8,128)(2,1)}, u32[]{:S(2)}, u32[]{:S(2)}) collective-permute-start(bf16[128,128]{1,0:T(8,128)(2,1)S(1)} %get-tuple-element.22), channel_id=1, source_target_pairs={{8,0},{16,8},{24,16},{32,24},{40,32},{48,40},{56,48},{64,56},{72,6... | collective-permute-start | bytes 98312 | tf_op jit(solution)/shard_map/ppermute | solution.py:19
  31.9 29.2 %collective-permute-start.9 = (bf16[128,128]{1,0:T(8,128)(2,1)S(1)}, bf16[128,128]{1,0:T(8,128)(2,1)S(1)}, u32[]{:S(2)}, u32[]{:S(2)}) collective-permute-start(bf16[128,128]{1,0:T(8,128)(2,1)S(1)} %get-tuple-element.23), channel_id=1, source_target_pairs={{8,0},{16,8},{24,16},{32,24},{40,32},{48,40},{56,48},{64,56},{72,6... | collective-permute-start | bytes 98312 | tf_op jit(solution)/shard_map/ppermute | solution.py:19
  34.8 20.1 %collective-permute-start.7 = (bf16[128,128]{1,0:T(8,128)(2,1)S(1)}, bf16[128,128]{1,0:T(8,128)(2,1)}, u32[]{:S(2)}, u32[]{:S(2)}) collective-permute-start(bf16[128,128]{1,0:T(8,128)(2,1)S(1)} %get-tuple-element.24), channel_id=1, source_target_pairs={{8,0},{16,8},{24,16},{32,24},{40,32},{48,40},{56,48},{64,56},{72,6... | collective-permute-start | bytes 98312 | tf_op jit(solution)/shard_map/ppermute | solution.py:19
  37.7 8.6 %collective-permute-start.3 = (bf16[128,128]{1,0:T(8,128)(2,1)S(1)}, bf16[128,128]{1,0:T(8,128)(2,1)}, u32[]{:S(2)}, u32[]{:S(2)}) collective-permute-start(bf16[128,128]{1,0:T(8,128)(2,1)S(1)} %get-tuple-element.27), channel_id=1, source_target_pairs={{0,8},{8,16},{16,24},{24,32},{32,40},{40,48},{48,56},{56,64},{64,7... | collective-permute-start | bytes 98312 | tf_op jit(solution)/shard_map/ppermute | solution.py:19
  42.6 7.9 %collective-permute-start.2 = (bf16[128,128]{1,0:T(8,128)(2,1)S(1)}, bf16[128,128]{1,0:T(8,128)(2,1)S(1)}, u32[]{:S(2)}, u32[]{:S(2)}) collective-permute-start(bf16[128,128]{1,0:T(8,128)(2,1)S(1)} %get-tuple-element.28), channel_id=1, source_target_pairs={{0,8},{8,16},{16,24},{24,32},{32,40},{40,48},{48,56},{56,64},{64,7... | collective-permute-start | bytes 98312 | tf_op jit(solution)/shard_map/ppermute | solution.py:19
  46.3 13.7 %collective-permute-start.6 = (bf16[128,128]{1,0:T(8,128)(2,1)S(1)}, bf16[128,128]{1,0:T(8,128)(2,1)S(1)}, u32[]{:S(2)}, u32[]{:S(2)}) collective-permute-start(bf16[128,128]{1,0:T(8,128)(2,1)S(1)} %get-tuple-element.25), channel_id=1, source_target_pairs={{1,0},{2,1},{3,2},{4,3},{5,4},{6,5},{7,6},{9,8},{10,9},{11,10},{12... | collective-permute-start | bytes 98312 | tf_op jit(solution)/shard_map/ppermute | solution.py:19
  50.5 5.7 %collective-permute-start.4 = (bf16[128,128]{1,0:T(8,128)(2,1)}, bf16[128,128]{1,0:T(8,128)(2,1)S(1)}, u32[]{:S(2)}, u32[]{:S(2)}) collective-permute-start(bf16[128,128]{1,0:T(8,128)(2,1)} %collective-permute-done.3), channel_id=1, source_target_pairs={{1,0},{2,1},{3,2},{4,3},{5,4},{6,5},{7,6},{9,8},{10,9},{11,10},{12... | collective-permute-start | bytes 98312 | tf_op jit(solution)/shard_map/ppermute | solution.py:19
  51.8 8.2 %collective-permute-start.5 = (bf16[128,128]{1,0:T(8,128)(2,1)S(1)}, bf16[128,128]{1,0:T(8,128)(2,1)S(1)}, u32[]{:S(2)}, u32[]{:S(2)}) collective-permute-start(bf16[128,128]{1,0:T(8,128)(2,1)S(1)} %get-tuple-element.26), channel_id=1, source_target_pairs={{0,1},{1,2},{2,3},{3,4},{4,5},{5,6},{6,7},{8,9},{9,10},{10,11},{11... | collective-permute-start | bytes 98312 | tf_op jit(solution)/shard_map/ppermute | solution.py:19
  54.9 6.2 %collective-permute-start.11 = (bf16[128,128]{1,0:T(8,128)(2,1)}, bf16[128,128]{1,0:T(8,128)(2,1)S(1)}, u32[]{:S(2)}, u32[]{:S(2)}) collective-permute-start(bf16[128,128]{1,0:T(8,128)(2,1)} %collective-permute-done.10), channel_id=1, source_target_pairs={{1,0},{2,1},{3,2},{4,3},{5,4},{6,5},{7,6},{9,8},{10,9},{11,10},{12... | collective-permute-start | bytes 98312 | tf_op jit(solution)/shard_map/ppermute | solution.py:19
  56.2 4.8 %collective-permute-start.8 = (bf16[128,128]{1,0:T(8,128)(2,1)}, bf16[128,128]{1,0:T(8,128)(2,1)S(1)}, u32[]{:S(2)}, u32[]{:S(2)}) collective-permute-start(bf16[128,128]{1,0:T(8,128)(2,1)} %collective-permute-done.7), channel_id=1, source_target_pairs={{0,1},{1,2},{2,3},{3,4},{4,5},{5,6},{6,7},{8,9},{9,10},{10,11},{11... | collective-permute-start | bytes 98312 | tf_op jit(solution)/shard_map/ppermute | solution.py:19
  65.3 0.7 copy-start.2
  88.4 143.9 %reduce-scatter.12.cloned.1.call-start = ((), (), s32[]{:S(2)}) async-start(), calls=%async_computation.7 | async-start | bytes 147456
  133.7 7.9 %collective-permute-start.12 = (bf16[128,128]{1,0:T(8,128)(2,1)S(1)}, bf16[128,128]{1,0:T(8,128)(2,1)S(1)}, u32[]{:S(2)}, u32[]{:S(2)}) collective-permute-start(bf16[128,128]{1,0:T(8,128)(2,1)S(1)} %get-tuple-element.21), channel_id=1, source_target_pairs={{0,8},{8,16},{16,24},{24,32},{32,40},{40,48},{48,56},{56,64},{64,7... | collective-permute-start | bytes 98312 | tf_op jit(solution)/shard_map/ppermute | solution.py:19
  141.6 13.6 %collective-permute-start.13 = (bf16[128,128]{1,0:T(8,128)(2,1)S(1)}, bf16[128,128]{1,0:T(8,128)(2,1)S(1)}, u32[]{:S(2)}, u32[]{:S(2)}) collective-permute-start(bf16[128,128]{1,0:T(8,128)(2,1)S(1)} %collective-permute-done.12), channel_id=1, source_target_pairs={{0,1},{1,2},{2,3},{3,4},{4,5},{5,6},{6,7},{8,9},{9,10},{10,11},{11... | collective-permute-start | bytes 98312 | tf_op jit(solution)/shard_map/ppermute | solution.py:19
  142.9 21.5 %collective-permute-start.22 = (bf16[128,128]{1,0:T(8,128)(2,1)S(1)}, bf16[128,128]{1,0:T(8,128)(2,1)S(1)}, u32[]{:S(2)}, u32[]{:S(2)}) collective-permute-start(bf16[128,128]{1,0:T(8,128)(2,1)S(1)} %get-tuple-element.14), channel_id=1, source_target_pairs={{8,0},{16,8},{24,16},{32,24},{40,32},{48,40},{56,48},{64,56},{72,6... | collective-permute-start | bytes 98312 | tf_op jit(solution)/shard_map/ppermute | solution.py:19
  146.0 27.4 %collective-permute-start.21 = (bf16[128,128]{1,0:T(8,128)(2,1)S(1)}, bf16[128,128]{1,0:T(8,128)(2,1)S(1)}, u32[]{:S(2)}, u32[]{:S(2)}) collective-permute-start(bf16[128,128]{1,0:T(8,128)(2,1)S(1)} %get-tuple-element.15), channel_id=1, source_target_pairs={{8,0},{16,8},{24,16},{32,24},{40,32},{48,40},{56,48},{64,56},{72,6... | collective-permute-start | bytes 98312 | tf_op jit(solution)/shard_map/ppermute | solution.py:19
  149.3 18.1 %collective-permute-start.19 = (bf16[128,128]{1,0:T(8,128)(2,1)S(1)}, bf16[128,128]{1,0:T(8,128)(2,1)S(1)}, u32[]{:S(2)}, u32[]{:S(2)}) collective-permute-start(bf16[128,128]{1,0:T(8,128)(2,1)S(1)} %get-tuple-element.16), channel_id=1, source_target_pairs={{8,0},{16,8},{24,16},{32,24},{40,32},{48,40},{56,48},{64,56},{72,6... | collective-permute-start | bytes 98312 | tf_op jit(solution)/shard_map/ppermute | solution.py:19
  152.6 8.0 %collective-permute-start.15 = (bf16[128,128]{1,0:T(8,128)(2,1)S(1)}, bf16[128,128]{1,0:T(8,128)(2,1)S(1)}, u32[]{:S(2)}, u32[]{:S(2)}) collective-permute-start(bf16[128,128]{1,0:T(8,128)(2,1)S(1)} %get-tuple-element.19), channel_id=1, source_target_pairs={{0,8},{8,16},{16,24},{24,32},{32,40},{40,48},{48,56},{56,64},{64,7... | collective-permute-start | bytes 98312 | tf_op jit(solution)/shard_map/ppermute | solution.py:19
  155.2 7.9 %collective-permute-start.14 = (bf16[128,128]{1,0:T(8,128)(2,1)S(1)}, bf16[128,128]{1,0:T(8,128)(2,1)S(1)}, u32[]{:S(2)}, u32[]{:S(2)}) collective-permute-start(bf16[128,128]{1,0:T(8,128)(2,1)S(1)} %get-tuple-element.20), channel_id=1, source_target_pairs={{0,8},{8,16},{16,24},{24,32},{32,40},{40,48},{48,56},{56,64},{64,7... | collective-permute-start | bytes 98312 | tf_op jit(solution)/shard_map/ppermute | solution.py:19
  160.6 11.9 %collective-permute-start.18 = (bf16[128,128]{1,0:T(8,128)(2,1)S(1)}, bf16[128,128]{1,0:T(8,128)(2,1)S(1)}, u32[]{:S(2)}, u32[]{:S(2)}) collective-permute-start(bf16[128,128]{1,0:T(8,128)(2,1)S(1)} %get-tuple-element.17), channel_id=1, source_target_pairs={{1,0},{2,1},{3,2},{4,3},{5,4},{6,5},{7,6},{9,8},{10,9},{11,10},{12... | collective-permute-start | bytes 98312 | tf_op jit(solution)/shard_map/ppermute | solution.py:19
  163.1 5.7 %collective-permute-start.16 = (bf16[128,128]{1,0:T(8,128)(2,1)S(1)}, bf16[128,128]{1,0:T(8,128)(2,1)S(1)}, u32[]{:S(2)}, u32[]{:S(2)}) collective-permute-start(bf16[128,128]{1,0:T(8,128)(2,1)S(1)} %collective-permute-done.15), channel_id=1, source_target_pairs={{1,0},{2,1},{3,2},{4,3},{5,4},{6,5},{7,6},{9,8},{10,9},{11,10},{12... | collective-permute-start | bytes 98312 | tf_op jit(solution)/shard_map/ppermute | solution.py:19
  164.4 8.1 %collective-permute-start.17 = (bf16[128,128]{1,0:T(8,128)(2,1)S(1)}, bf16[128,128]{1,0:T(8,128)(2,1)S(1)}, u32[]{:S(2)}, u32[]{:S(2)}) collective-permute-start(bf16[128,128]{1,0:T(8,128)(2,1)S(1)} %get-tuple-element.18), channel_id=1, source_target_pairs={{0,1},{1,2},{2,3},{3,4},{4,5},{5,6},{6,7},{8,9},{9,10},{10,11},{11... | collective-permute-start | bytes 98312 | tf_op jit(solution)/shard_map/ppermute | solution.py:19
  167.4 5.9 %collective-permute-start.23 = (bf16[128,128]{1,0:T(8,128)(2,1)S(1)}, bf16[128,128]{1,0:T(8,128)(2,1)S(1)}, u32[]{:S(2)}, u32[]{:S(2)}) collective-permute-start(bf16[128,128]{1,0:T(8,128)(2,1)S(1)} %collective-permute-done.22), channel_id=1, source_target_pairs={{1,0},{2,1},{3,2},{4,3},{5,4},{6,5},{7,6},{9,8},{10,9},{11,10},{12... | collective-permute-start | bytes 98312 | tf_op jit(solution)/shard_map/ppermute | solution.py:19
  168.8 4.6 %collective-permute-start.20 = (bf16[128,128]{1,0:T(8,128)(2,1)S(1)}, bf16[128,128]{1,0:T(8,128)(2,1)S(1)}, u32[]{:S(2)}, u32[]{:S(2)}) collective-permute-start(bf16[128,128]{1,0:T(8,128)(2,1)S(1)} %collective-permute-done.19), channel_id=1, source_target_pairs={{0,1},{1,2},{2,3},{3,4},{4,5},{5,6},{6,7},{8,9},{9,10},{10,11},{11... | collective-permute-start | bytes 98312 | tf_op jit(solution)/shard_map/ppermute | solution.py:19
  177.7 0.7 copy-start.3
  200.4 141.3 %reduce-scatter.14.cloned.1.call-start = ((), (), s32[]{:S(2)}) async-start(), calls=%async_computation.8 | async-start | bytes 147456
  240.6 43.1 %copy-start.1 = (bf16[1536,128]{0,1:T(8,128)(2,1)}, bf16[1536,128]{0,1:T(8,128)(2,1)S(1)}, u32[]{:S(2)}) copy-start(bf16[1536,128]{0,1:T(8,128)(2,1)S(1)} %fusion.48) | copy-start | bytes 1179652
  242.9 7.9 %collective-permute-start.24 = (bf16[128,128]{1,0:T(8,128)(2,1)S(1)}, bf16[128,128]{1,0:T(8,128)(2,1)S(1)}, u32[]{:S(2)}, u32[]{:S(2)}) collective-permute-start(bf16[128,128]{1,0:T(8,128)(2,1)S(1)} %get-tuple-element.13), channel_id=1, source_target_pairs={{0,8},{8,16},{16,24},{24,32},{32,40},{40,48},{48,56},{56,64},{64,7... | collective-permute-start | bytes 98312 | tf_op jit(solution)/shard_map/ppermute | solution.py:19
  250.8 13.6 %collective-permute-start.25 = (bf16[128,128]{1,0:T(8,128)(2,1)S(1)}, bf16[128,128]{1,0:T(8,128)(2,1)S(1)}, u32[]{:S(2)}, u32[]{:S(2)}) collective-permute-start(bf16[128,128]{1,0:T(8,128)(2,1)S(1)} %collective-permute-done.24), channel_id=1, source_target_pairs={{0,1},{1,2},{2,3},{3,4},{4,5},{5,6},{6,7},{8,9},{9,10},{10,11},{11... | collective-permute-start | bytes 98312 | tf_op jit(solution)/shard_map/ppermute | solution.py:19
  252.1 21.5 %collective-permute-start.34 = (bf16[128,128]{1,0:T(8,128)(2,1)S(1)}, bf16[128,128]{1,0:T(8,128)(2,1)S(1)}, u32[]{:S(2)}, u32[]{:S(2)}) collective-permute-start(bf16[128,128]{1,0:T(8,128)(2,1)S(1)} %get-tuple-element.6), channel_id=1, source_target_pairs={{8,0},{16,8},{24,16},{32,24},{40,32},{48,40},{56,48},{64,56},{72,6... | collective-permute-start | bytes 98312 | tf_op jit(solution)/shard_map/ppermute | solution.py:19
  255.3 27.4 %collective-permute-start.33 = (bf16[128,128]{1,0:T(8,128)(2,1)S(1)}, bf16[128,128]{1,0:T(8,128)(2,1)S(1)}, u32[]{:S(2)}, u32[]{:S(2)}) collective-permute-start(bf16[128,128]{1,0:T(8,128)(2,1)S(1)} %get-tuple-element.7), channel_id=1, source_target_pairs={{8,0},{16,8},{24,16},{32,24},{40,32},{48,40},{56,48},{64,56},{72,6... | collective-permute-start | bytes 98312 | tf_op jit(solution)/shard_map/ppermute | solution.py:19
  258.5 18.1 %collective-permute-start.31 = (bf16[128,128]{1,0:T(8,128)(2,1)S(1)}, bf16[128,128]{1,0:T(8,128)(2,1)S(1)}, u32[]{:S(2)}, u32[]{:S(2)}) collective-permute-start(bf16[128,128]{1,0:T(8,128)(2,1)S(1)} %get-tuple-element.8), channel_id=1, source_target_pairs={{8,0},{16,8},{24,16},{32,24},{40,32},{48,40},{56,48},{64,56},{72,6... | collective-permute-start | bytes 98312 | tf_op jit(solution)/shard_map/ppermute | solution.py:19
  261.9 8.0 %collective-permute-start.27 = (bf16[128,128]{1,0:T(8,128)(2,1)S(1)}, bf16[128,128]{1,0:T(8,128)(2,1)S(1)}, u32[]{:S(2)}, u32[]{:S(2)}) collective-permute-start(bf16[128,128]{1,0:T(8,128)(2,1)S(1)} %get-tuple-element.11), channel_id=1, source_target_pairs={{0,8},{8,16},{16,24},{24,32},{32,40},{40,48},{48,56},{56,64},{64,7... | collective-permute-start | bytes 98312 | tf_op jit(solution)/shard_map/ppermute | solution.py:19
  264.4 7.9 %collective-permute-start.26 = (bf16[128,128]{1,0:T(8,128)(2,1)S(1)}, bf16[128,128]{1,0:T(8,128)(2,1)S(1)}, u32[]{:S(2)}, u32[]{:S(2)}) collective-permute-start(bf16[128,128]{1,0:T(8,128)(2,1)S(1)} %get-tuple-element.12), channel_id=1, source_target_pairs={{0,8},{8,16},{16,24},{24,32},{32,40},{40,48},{48,56},{56,64},{64,7... | collective-permute-start | bytes 98312 | tf_op jit(solution)/shard_map/ppermute | solution.py:19
  269.9 11.9 %collective-permute-start.30 = (bf16[128,128]{1,0:T(8,128)(2,1)S(1)}, bf16[128,128]{1,0:T(8,128)(2,1)S(1)}, u32[]{:S(2)}, u32[]{:S(2)}) collective-permute-start(bf16[128,128]{1,0:T(8,128)(2,1)S(1)} %get-tuple-element.9), channel_id=1, source_target_pairs={{1,0},{2,1},{3,2},{4,3},{5,4},{6,5},{7,6},{9,8},{10,9},{11,10},{12... | collective-permute-start | bytes 98312 | tf_op jit(solution)/shard_map/ppermute | solution.py:19
  272.3 5.7 %collective-permute-start.28 = (bf16[128,128]{1,0:T(8,128)(2,1)S(1)}, bf16[128,128]{1,0:T(8,128)(2,1)S(1)}, u32[]{:S(2)}, u32[]{:S(2)}) collective-permute-start(bf16[128,128]{1,0:T(8,128)(2,1)S(1)} %collective-permute-done.27), channel_id=1, source_target_pairs={{1,0},{2,1},{3,2},{4,3},{5,4},{6,5},{7,6},{9,8},{10,9},{11,10},{12... | collective-permute-start | bytes 98312 | tf_op jit(solution)/shard_map/ppermute | solution.py:19
  273.6 8.2 %collective-permute-start.29 = (bf16[128,128]{1,0:T(8,128)(2,1)S(1)}, bf16[128,128]{1,0:T(8,128)(2,1)S(1)}, u32[]{:S(2)}, u32[]{:S(2)}) collective-permute-start(bf16[128,128]{1,0:T(8,128)(2,1)S(1)} %get-tuple-element.10), channel_id=1, source_target_pairs={{0,1},{1,2},{2,3},{3,4},{4,5},{5,6},{6,7},{8,9},{9,10},{10,11},{11... | collective-permute-start | bytes 98312 | tf_op jit(solution)/shard_map/ppermute | solution.py:19
  276.7 6.0 %collective-permute-start.35 = (bf16[128,128]{1,0:T(8,128)(2,1)S(1)}, bf16[128,128]{1,0:T(8,128)(2,1)S(1)}, u32[]{:S(2)}, u32[]{:S(2)}) collective-permute-start(bf16[128,128]{1,0:T(8,128)(2,1)S(1)} %collective-permute-done.34), channel_id=1, source_target_pairs={{1,0},{2,1},{3,2},{4,3},{5,4},{6,5},{7,6},{9,8},{10,9},{11,10},{12... | collective-permute-start | bytes 98312 | tf_op jit(solution)/shard_map/ppermute | solution.py:19
  278.0 4.7 %collective-permute-start.32 = (bf16[128,128]{1,0:T(8,128)(2,1)S(1)}, bf16[128,128]{1,0:T(8,128)(2,1)S(1)}, u32[]{:S(2)}, u32[]{:S(2)}) collective-permute-start(bf16[128,128]{1,0:T(8,128)(2,1)S(1)} %collective-permute-done.31), channel_id=1, source_target_pairs={{0,1},{1,2},{2,3},{3,4},{4,5},{5,6},{6,7},{8,9},{9,10},{10,11},{11... | collective-permute-start | bytes 98312 | tf_op jit(solution)/shard_map/ppermute | solution.py:19
Sparse Core Ops, SparseCore 0:
  88.5 34.6 reduce-scatter.9
  200.5 31.7 reduce-scatter.11
  309.8 31.8 reduce-scatter.13
